TPU v7x, 32 devices: a whole 2x2x4 slice. The times are simulated.
32 devices in a mesh: gx: 4 (over y, core), gy: 8 (over z, x).
Axes of the slice: x: 2, y: 2, z: 4, core: 2. Of those that a mesh axis runs over, the one named last changes fastest.
Arguments:
- tokens: bfloat16 [4, 256, 6144], P('gx', None, 'gy'), may hold values from -6 to 6
- norm_gain: float32 [6144], replicated, may hold values from 0.1 to 1.9
- qkv_weight: bfloat16 [6144, 3, 4096], P('gx', None, 'gy'), may hold values from -0.078125 to 0.078125
- up_weight: bfloat16 [6144, 24576], P('gx', 'gy'), may hold values from -0.078125 to 0.078125
- query_gain: float32 [128], replicated, may hold values from 0.1 to 1.9
- key_gain: float32 [128], replicated, may hold values from 0.1 to 1.9
- out_weight: bfloat16 [4096, 6144], P('gy', 'gx'), may hold values from -0.09375 to 0.09375
- down_weight: bfloat16 [24576, 6144], P('gy', 'gx'), may hold values from -0.0390625 to 0.0390625
- attention_keep: int32 [4, 256, 6144], P('gx', None, 'gy'), may hold values 0 or 1
- feedforward_keep: int32 [4, 256, 6144], P('gx', None, 'gy'), may hold values 0 or 1
Outputs:
- block_out: bfloat16 [4, 256, 6144], P('gx', None, 'gy')
All inputs are finite; a program needn't handle non-finite values. No bound on the sum of `attention_keep` or of `feedforward_keep` on one device may be relied on, other than what follows from the above.
Results may differ from a plain program's by a relative error of at most 0.017.
Values may be sent and summed in bfloat16 or wider, within the bound.
A program may use at most 128 MiB of HBM per device.

v0:
```python
import jax
import jax.numpy as jnp
from jax import lax
from jax.sharding import PartitionSpec as P

epsilon = 1e-06
keep_scale = 1.0 / 0.9


def layer_norm(values, gain):
    center = values - jnp.mean(values, axis=-1, keepdims=True)
    variance = jnp.mean(center * center, axis=-1, keepdims=True)
    return center * lax.rsqrt(variance + epsilon) * gain


def head_norm(values, gain):
    row_count = values.shape[0]
    shaped = values.reshape(row_count, -1, gain.shape[0])
    return layer_norm(shaped, gain).reshape(row_count, -1)


def per_device(
    tokens,
    norm_gain,
    qkv_weight,
    up_weight,
    query_gain,
    key_gain,
    out_weight,
    down_weight,
    attention_keep,
    feedforward_keep,
):
    images, seq_len, slice_width = tokens.shape
    whole_rows = lax.all_gather(tokens, "gy", axis=2, tiled=True)
    model_width = whole_rows.shape[2]
    own_rows = images * seq_len
    normed = (
        layer_norm(whole_rows.astype(jnp.float32), norm_gain)
        .astype(jnp.bfloat16)
        .reshape(own_rows, model_width)
    )
    blocks = lax.all_to_all(normed, "gx", split_axis=1, concat_axis=0, tiled=True)
    block_width = blocks.shape[1]
    head_cols = qkv_weight.shape[2]
    head_size = query_gain.shape[0]
    qkv_flat = qkv_weight.reshape(block_width, 3 * head_cols)
    joined = jnp.concatenate([qkv_flat, up_weight], axis=1)
    united = lax.psum_scatter(
        jnp.dot(blocks, joined, preferred_element_type=jnp.float32).astype(jnp.bfloat16),
        "gx",
        scatter_dimension=0,
        tiled=True,
    ).astype(jnp.float32)
    queries = head_norm(united[:, :head_cols], query_gain).astype(jnp.bfloat16)
    keys = head_norm(united[:, head_cols : 2 * head_cols], key_gain).astype(jnp.bfloat16)
    values = united[:, 2 * head_cols : 3 * head_cols].astype(jnp.bfloat16)
    hidden = jax.nn.gelu(united[:, 3 * head_cols :], approximate=False).astype(jnp.bfloat16)
    query_grid = queries.reshape(images, seq_len, -1, head_size)
    key_grid = keys.reshape(images, seq_len, -1, head_size)
    value_grid = values.reshape(images, seq_len, -1, head_size)
    scores = jnp.einsum(
        "bshd,bthd->bhst", query_grid, key_grid, preferred_element_type=jnp.float32
    ) * head_size ** (-0.5)
    raised = jnp.exp(scores)
    weights = (raised / jnp.sum(raised, axis=-1, keepdims=True)).astype(jnp.bfloat16)
    attended = jnp.einsum(
        "bhst,bthd->bshd", weights, value_grid, preferred_element_type=jnp.float32
    )
    attended = attended.astype(jnp.bfloat16).reshape(own_rows, head_cols)
    attention_part = jnp.dot(
        lax.all_gather(attended, "gx", axis=0, tiled=True),
        out_weight,
        preferred_element_type=jnp.float32,
    )
    feedforward_part = jnp.dot(
        lax.all_gather(hidden, "gx", axis=0, tiled=True),
        down_weight,
        preferred_element_type=jnp.float32,
    )
    delivered = (
        lax.all_to_all(
            attention_part.astype(jnp.bfloat16), "gx", split_axis=0, concat_axis=1, tiled=True
        ),
        lax.all_to_all(
            feedforward_part.astype(jnp.bfloat16), "gx", split_axis=0, concat_axis=1, tiled=True
        ),
    )
    rounded = jnp.stack([delivered[0], delivered[1]])
    rounded = lax.optimization_barrier(rounded)
    totals = lax.psum_scatter(
        rounded.astype(jnp.float32).astype(jnp.bfloat16), "gy", scatter_dimension=2, tiled=True
    ).astype(jnp.float32)
    attention_out = totals[0].reshape(images, seq_len, slice_width)
    feedforward_out = totals[1].reshape(images, seq_len, slice_width)
    branches = (
        attention_keep.astype(jnp.float32) * attention_out
        + feedforward_keep.astype(jnp.float32) * feedforward_out
    )
    return (tokens.astype(jnp.float32) + branches * keep_scale).astype(jnp.bfloat16)


def solution(mesh):
    in_specs = (
        P("gx", None, "gy"),
        P(),
        P("gx", None, "gy"),
        P("gx", "gy"),
        P(),
        P(),
        P("gy", "gx"),
        P("gy", "gx"),
        P("gx", None, "gy"),
        P("gx", None, "gy"),
    )
    out_specs = P("gx", None, "gy")
    return jax.shard_map(
        per_device, mesh=mesh, in_specs=in_specs, out_specs=out_specs, check_vma=False
    )
```

profile of v0, /device:TPU:0, one launch (start us, length us, event | category | flops | bytes accessed | tf_op | source)
XLA Modules:
  0.0 534.5 jit_solution(1531559722905003716)
XLA Ops:
  6.5 2.0 copy.26
  8.6 63.7 %all-gather.4.cloned.1.call-done = bf16[1,256,6144]{1,2,0:T(8,128)(2,1)} async-done(((bf16[1,256,768]{1,2,0:T(8,128)(2,1)}), bf16[1,256,6144]{1,2,0:T(8,128)(2,1)}) %all-gather.4.cloned.1.call-update) | async-done | bytes 3145744 | tf_op jit(solution)/shard_map/all_gather | solution.py:35
  72.3 2.9 convert_reduce_fusion
  75.2 0.9 fusion.9
  76.1 2.3 fusion.11
  78.3 4.7 all-to-all-start
  83.1 6.6 %copy.28 = bf16[1536,3,512]{0,2,1:T(8,128)(2,1)} copy(bf16[1536,3,512]{2,0,1:T(8,128)(2,1)} %param.12) | data formatting | bytes 9437184 | tf_op args[2]
  89.7 6.6 %copy.29 = bf16[1536,1536]{1,0:T(8,128)(2,1)} copy(bf16[1536,1536]{0,1:T(8,128)(2,1)} %bitcast.67) | data formatting | bytes 9437184 | tf_op jit(solution)/shard_map/reshape | solution.py:47
  96.3 23.7 %all-to-all-done = bf16[256,4,1536]{0,2,1:T(8,128)(2,1)} async-done(((bf16[256,4,1536]{0,2,1:T(8,128)(2,1)}), bf16[256,4,1536]{0,2,1:T(8,128)(2,1)}, u32[]{:S(2)}, u32[]{:S(2)}) %all-to-all-start) | async-done | bytes 3145760 | tf_op jit(solution)/shard_map/all_to_all | solution.py:43
  120.0 4.7 copy.27
  124.6 22.6 %fusion.4 = bf16[1024,4608]{1,0:T(8,128)(2,1)} fusion(bf16[1024,1536]{1,0:T(8,128)(2,1)} %bitcast.71, bf16[1536,3072]{1,0:T(8,128)(2,1)} %param.13, bf16[1536,1536]{1,0:T(8,128)(2,1)} %copy.29), kind=kOutput, calls=%fused_computation.4 | convolution fusion | flops 14528544768 | bytes 26738688 | tf_op jit(solution)/shard_map/dot_general | solution.py:50
  148.0 75.2 %reduce-scatter.3.cloned.1.call-done = bf16[256,4608]{1,0:T(8,128)(2,1)} async-done(((bf16[1024,4608]{1,0:T(8,128)(2,1)}), bf16[256,4608]{1,0:T(8,128)(2,1)}) %reduce-scatter.3.cloned.1.call-update) | async-done | bytes 2359312 | tf_op jit(solution)/shard_map/reduce_scatter | solution.py:49
  223.2 1.2 fusion.40
  224.9 0.6 multiply_reduce_fusion
  227.0 2.2 convert_element_type.63
  231.6 1.0 convolution_convert_fusion.2
  232.7 8.6 %fusion.14 = bf16[256,3072]{1,0:T(8,128)(2,1)} fusion(f32[256,4608]{1,0:T(8,128)} %copy-done.3), kind=kLoop, calls=%fused_computation.18 | loop fusion | flops 51118080 | bytes 4718592 | tf_op jit(solution)/shard_map/convert_element_type | solution.py:58
  241.3 8.3 %all-gather.6.cloned.1.call-done = bf16[1024,512]{0,1:T(8,128)(2,1)} async-done(((bf16[256,512]{0,1:T(8,128)(2,1)}), bf16[1024,512]{0,1:T(8,128)(2,1)}) %all-gather.6.cloned.1.call-update) | async-done | bytes 1048592 | tf_op jit(solution)/shard_map/all_gather | solution.py:72
  249.6 4.7 convolution_convert_fusion.1
  254.3 4.7 all-to-all-start.1
  259.1 72.0 %all-gather.8.cloned.1.call-done = bf16[1024,3072]{1,0:T(8,128)(2,1)} async-done(((bf16[256,3072]{1,0:T(8,128)(2,1)}), bf16[1024,3072]{1,0:T(8,128)(2,1)}) %all-gather.8.cloned.1.call-update) | async-done | bytes 6291472 | tf_op jit(solution)/shard_map/all_gather | solution.py:77
  331.1 15.6 %convolution_convert_fusion = bf16[1024,1536]{1,0:T(8,128)(2,1)} fusion(bf16[1024,3072]{1,0:T(8,128)(2,1)} %all-gather.8.cloned.1.call-done, bf16[3072,1536]{1,0:T(8,128)(2,1)} %param.17), kind=kOutput, calls=%fused_computation.14 | convolution fusion | flops 9665249280 | bytes 18874368 | tf_op jit(solution)/shard_map/dot_general | solution.py:76
  346.6 4.9 all-to-all-start.2
  351.6 6.0 %copy.34 = bf16[256,4,1536]{2,1,0:T(4,128)(2,1)} copy(bf16[256,4,1536]{2,0,1:T(8,128)(2,1)} %bitcast.11) | data formatting | bytes 6291456 | tf_op jit(solution)/shard_map/all_to_all | solution.py:82
  357.6 6.9 %stack.9 = bf16[1,256,6144]{2,1,0:T(8,128)(2,1)} reshape(bf16[256,4,1536]{2,1,0:T(4,128)(2,1)} %copy.34) | data formatting | bytes 6291456 | tf_op jit(solution)/shard_map/stack | solution.py:89
  364.5 24.0 %all-to-all-done.2 = bf16[4,256,1536]{2,1,0:T(8,128)(2,1)} async-done(((bf16[4,256,1536]{2,1,0:T(8,128)(2,1)}), bf16[4,256,1536]{2,1,0:T(8,128)(2,1)}, u32[]{:S(2)}, u32[]{:S(2)}) %all-to-all-start.2) | async-done | bytes 3145760 | tf_op jit(solution)/shard_map/all_to_all | solution.py:85
  388.5 6.0 %copy.35 = bf16[256,4,1536]{2,1,0:T(4,128)(2,1)} copy(bf16[256,4,1536]{2,0,1:T(8,128)(2,1)} %bitcast.13) | data formatting | bytes 6291456 | tf_op jit(solution)/shard_map/all_to_all | solution.py:85
  394.5 6.9 %stack.10 = bf16[1,256,6144]{2,1,0:T(8,128)(2,1)} reshape(bf16[256,4,1536]{2,1,0:T(4,128)(2,1)} %copy.35) | data formatting | bytes 6291456 | tf_op jit(solution)/shard_map/stack | solution.py:89
  401.4 6.1 %pad_maximum_fusion = bf16[2,256,6144]{2,1,0:T(8,128)(2,1)} fusion(bf16[1,256,6144]{2,1,0:T(8,128)(2,1)} %stack.10, bf16[1,256,6144]{2,1,0:T(8,128)(2,1)} %stack.9), kind=kLoop, calls=%fused_computation.12 | loop fusion | flops 3145728 | bytes 12582912 | tf_op jit(solution)/shard_map/stack | solution.py:89
  407.5 118.2 %reduce-scatter.5.cloned.1.call-done = bf16[2,256,768]{2,1,0:T(8,128)(2,1)} async-done(((bf16[2,256,6144]{2,1,0:T(8,128)(2,1)}), bf16[2,256,768]{2,1,0:T(8,128)(2,1)}) %reduce-scatter.5.cloned.1.call-update) | async-done | bytes 786448 | tf_op jit(solution)/shard_map/reduce_scatter | solution.py:91
  525.7 1.2 convert_element_type.73
  527.0 1.0 fusion.26
  (52 shorter events, 5.2 us)
Async XLA Ops:
  6.5 243.1 %copy-start = (bf16[512,1536]{1,0:T(8,128)(2,1)S(1)}, bf16[512,1536]{1,0:T(8,128)(2,1)}, u32[]{:S(2)}) copy-start(bf16[512,1536]{1,0:T(8,128)(2,1)} %param.16) | copy-start | bytes 4718596
  6.5 65.7 %all-gather.4.cloned.1.call-start = ((), (), s32[]{:S(2)}) async-start(), calls=%async_computation.5 | async-start | bytes 3538944 | tf_op jit(solution)/shard_map/all_gather | solution.py:35
  72.3 2.9 copy-start.2
  72.3 3.8 copy-start.7
  78.3 41.7 %all-to-all-start = ((bf16[256,4,1536]{0,2,1:T(8,128)(2,1)}), bf16[256,4,1536]{0,2,1:T(8,128)(2,1)}, u32[]{:S(2)}, u32[]{:S(2)}) async-start(bf16[256,4,1536]{0,2,1:T(8,128)(2,1)} %bitcast.68), calls=%async_computation | async-start | bytes 6291456 | tf_op jit(solution)/shard_map/all_to_all | solution.py:43
  83.0 140.2 %reduce-scatter.3.cloned.1.call-start = ((), (), s32[]{:S(2)}) async-start(), calls=%async_computation.6 | async-start | bytes 11796480 | tf_op jit(solution)/shard_map/reduce_scatter | solution.py:49
  147.3 0.7 copy-start.8
  147.3 0.7 copy-start.9
  147.3 102.3 %all-gather.6.cloned.1.call-start = ((), (), s32[]{:S(2)}) async-start(), calls=%async_computation.7 | async-start | bytes 1310720 | tf_op jit(solution)/shard_map/all_gather | solution.py:72
  224.3 2.5 slice-start
  229.2 2.1 copy-start.3
  232.7 98.4 %all-gather.8.cloned.1.call-start = ((), (), s32[]{:S(2)}) async-start(), calls=%async_computation.8 | async-start | bytes 7864320 | tf_op jit(solution)/shard_map/all_gather | solution.py:77
  254.3 92.3 %all-to-all-start.1 = ((bf16[4,256,1536]{2,1,0:T(8,128)(2,1)}), bf16[4,256,1536]{2,1,0:T(8,128)(2,1)}, u32[]{:S(2)}, u32[]{:S(2)}) async-start(bf16[4,256,1536]{2,1,0:T(8,128)(2,1)} %bitcast.70), calls=%async_computation.2 | async-start | bytes 6291456 | tf_op jit(solution)/shard_map/all_to_all | solution.py:82
  346.6 41.8 %all-to-all-start.2 = ((bf16[4,256,1536]{2,1,0:T(8,128)(2,1)}), bf16[4,256,1536]{2,1,0:T(8,128)(2,1)}, u32[]{:S(2)}, u32[]{:S(2)}) async-start(bf16[4,256,1536]{2,1,0:T(8,128)(2,1)} %bitcast.69), calls=%async_computation.3 | async-start | bytes 6291456 | tf_op jit(solution)/shard_map/all_to_all | solution.py:85
  351.5 174.2 %reduce-scatter.5.cloned.1.call-start = ((), (), s32[]{:S(2)}) async-start(), calls=%async_computation.9 | async-start | bytes 7077888 | tf_op jit(solution)/shard_map/reduce_scatter | solution.py:91
  407.5 119.4 %copy-start.4 = (bf16[1,256,768]{2,1,0:T(8,128)(2,1)S(1)}, bf16[1,256,768]{2,1,0:T(8,128)(2,1)}, u32[]{:S(2)}) copy-start(bf16[1,256,768]{2,1,0:T(8,128)(2,1)} %param.10) | copy-start | bytes 1179652
  407.5 119.5 %copy-start.5 = (s32[1,256,768]{2,1,0:T(8,128)S(1)}, s32[1,256,768]{2,1,0:T(8,128)}, u32[]{:S(2)}) copy-start(s32[1,256,768]{2,1,0:T(8,128)} %param.19) | copy-start | bytes 2359300
  407.5 119.5 %copy-start.6 = (s32[1,256,768]{2,1,0:T(8,128)S(1)}, s32[1,256,768]{2,1,0:T(8,128)}, u32[]{:S(2)}) copy-start(s32[1,256,768]{2,1,0:T(8,128)} %param.18) | copy-start | bytes 2359300
  407.5 120.4 %copy-start.1 = (bf16[512,1536]{1,0:T(8,128)(2,1)S(1)}, bf16[512,1536]{1,0:T(8,128)(2,1)}, u32[]{:S(2)}) copy-start(bf16[512,1536]{1,0:T(8,128)(2,1)} %param.16) | copy-start | bytes 4718596
Sparse Core Ops, SparseCore 0:
  9.5 62.7 all-gather.3
  147.4 75.6 reduce-scatter.2
  232.8 16.8 all-gather.5
  251.0 79.9 all-gather.7
  407.6 118.0 reduce-scatter.4
where the time goes:
time: 536 us; the launch traced here: 534 us
  waiting for transfers between devices  385 us (72%)
  local copies, waits for them, and re-layouts  49.6 us (9%)
  matrix products  44.2 us (8%)
  other arithmetic  27.6 us (5%)
  starting transfers between devices  14.6 us (3%)
  between operations  13.4 us (2%)
    reduce_scatter x1, waiting for transfers between devices, per_device(): lax.psum_scatter(rounded.astype(jnp.float32).astype(jnp.bfloat16), 'gy',...  118 us
    reduce_scatter x1, waiting for transfers between devices, per_device(): lax.psum_scatter(jnp.dot(blocks, joined, preferred_element_type=jnp.float...  75.2 us
    all_gather x1, waiting for transfers between devices, per_device(): lax.all_gather(hidden, 'gx', axis=0, tiled=True)  72 us
    all_gather x1, waiting for transfers between devices, per_device(): whole_rows = lax.all_gather(tokens, 'gy', axis=2, tiled=True)  63.7 us
    all_to_all x1, waiting for transfers between devices, per_device(): lax.all_to_all(feedforward_part.astype(jnp.bfloat16), 'gx', split_axis=0,...  24 us
    all_to_all x1, waiting for transfers between devices, per_device(): lax.all_to_all(normed, 'gx', split_axis=1, concat_axis=0, tiled=True)  23.7 us
    dot_general x1, matrix products, per_device(): jnp.dot(blocks, joined, preferred_element_type=jnp.float32)  22.6 us
    dot_general x1, matrix products, per_device(): jnp.dot(lax.all_gather(hidden, 'gx', axis=0, tiled=True), down_weight, pr...  15.6 us
  transfers between devices with their start and end apart: 8, of which 7 were waited for; matrix products, arithmetic and copies ran while one was open for 10% of the time, Pallas kernels for 0%

commit v1 on v0

--- a/solution.py
+++ b/solution.py
@@ -32,7 +32,13 @@
     feedforward_keep,
 ):
     images, seq_len, slice_width = tokens.shape
-    whole_rows = lax.all_gather(tokens, "gy", axis=2, tiled=True)
+
+    def wait_zone(frame_in, axis_key, along_dim):
+        carry = lax.all_gather(frame_in, axis_key)
+        z2 = jnp.concatenate(carry, along_dim)
+        return z2
+
+    whole_rows = wait_zone(tokens, "gy", 2)
     model_width = whole_rows.shape[2]
     own_rows = images * seq_len
     normed = (

time: 536 us -> 541 us (level)
  no operation moved by 1% of the time
where the time goes in v1:
time: 541 us; the launch traced here: 540 us
  waiting for transfers between devices  386 us (71%)
  local copies, waits for them, and re-layouts  53.3 us (10%)
  matrix products  44.2 us (8%)
  other arithmetic  28 us (5%)
  starting transfers between devices  14.6 us (3%)
  between operations  13.4 us (2%)
    reduce_scatter x1, waiting for transfers between devices, per_device(): lax.psum_scatter(rounded.astype(jnp.float32).astype(jnp.bfloat16), 'gy',...  118 us
    reduce_scatter x1, waiting for transfers between devices, per_device(): lax.psum_scatter(jnp.dot(blocks, joined, preferred_element_type=jnp.float...  75.2 us
    all_gather x1, waiting for transfers between devices, per_device(): lax.all_gather(hidden, 'gx', axis=0, tiled=True)  72 us
    all_gather x1, waiting for transfers between devices, wait_zone(): carry = lax.all_gather(frame_in, axis_key)  64.3 us
    all_to_all x1, waiting for transfers between devices, per_device(): lax.all_to_all(feedforward_part.astype(jnp.bfloat16), 'gx', split_axis=0,...  24 us
    all_to_all x1, waiting for transfers between devices, per_device(): lax.all_to_all(normed, 'gx', split_axis=1, concat_axis=0, tiled=True)  23.6 us
    dot_general x1, matrix products, per_device(): jnp.dot(blocks, joined, preferred_element_type=jnp.float32)  22.7 us
    dot_general x1, matrix products, per_device(): jnp.dot(lax.all_gather(hidden, 'gx', axis=0, tiled=True), down_weight, pr...  15.5 us
  transfers between devices with their start and end apart: 8, of which 7 were waited for; matrix products, arithmetic and copies ran while one was open for 10% of the time, Pallas kernels for 0%

profile of v1, /device:TPU:0, one launch (start us, length us, event | category | flops | bytes accessed | tf_op | source)
XLA Modules:
  0.0 539.8 jit_solution(11545328693688601916)
XLA Ops:
  8.0 64.3 %all-gather.9.cloned.1.call-done = bf16[8,256,768]{2,1,0:T(8,128)(2,1)} async-done(((bf16[1,256,768]{2,1,0:T(8,128)(2,1)}), bf16[8,256,768]{2,1,0:T(8,128)(2,1)}) %all-gather.9.cloned.1.call-update) | async-done | bytes 3145744 | tf_op jit(solution)/shard_map/all_gather | solution.py:37
  72.3 4.7 copy.28
  76.9 2.6 convert_element_type.118
  79.8 0.8 convert_reduce_fusion
  80.6 0.8 fusion.8
  81.5 2.2 multiply_convert_fusion
  83.6 4.7 all-to-all-start
  88.4 6.7 %copy.30 = bf16[1536,3,512]{0,2,1:T(8,128)(2,1)} copy(bf16[1536,3,512]{2,0,1:T(8,128)(2,1)} %param.12) | data formatting | bytes 9437184 | tf_op args[2]
  95.0 6.6 %copy.31 = bf16[1536,1536]{1,0:T(8,128)(2,1)} copy(bf16[1536,1536]{0,1:T(8,128)(2,1)} %bitcast.81) | data formatting | bytes 9437184 | tf_op jit(solution)/shard_map/reshape | solution.py:53
  101.6 23.6 %all-to-all-done = bf16[256,4,1536]{0,2,1:T(8,128)(2,1)} async-done(((bf16[256,4,1536]{0,2,1:T(8,128)(2,1)}), bf16[256,4,1536]{0,2,1:T(8,128)(2,1)}, u32[]{:S(2)}, u32[]{:S(2)}) %all-to-all-start) | async-done | bytes 3145760 | tf_op jit(solution)/shard_map/all_to_all | solution.py:49
  125.3 4.7 copy.29
  130.0 22.7 %fusion.4 = bf16[1024,4608]{1,0:T(8,128)(2,1)} fusion(bf16[1024,1536]{1,0:T(8,128)(2,1)} %bitcast.84, bf16[1536,3072]{1,0:T(8,128)(2,1)} %param.13, bf16[1536,1536]{1,0:T(8,128)(2,1)} %copy.31), kind=kOutput, calls=%fused_computation.4 | convolution fusion | flops 14528544768 | bytes 26738688 | tf_op jit(solution)/shard_map/dot_general | solution.py:56
  153.3 75.2 %reduce-scatter.3.cloned.1.call-done = bf16[256,4608]{1,0:T(8,128)(2,1)} async-done(((bf16[1024,4608]{1,0:T(8,128)(2,1)}), bf16[256,4608]{1,0:T(8,128)(2,1)}) %reduce-scatter.3.cloned.1.call-update) | async-done | bytes 2359312 | tf_op jit(solution)/shard_map/reduce_scatter | solution.py:55
  228.5 1.2 fusion.37
  232.3 2.2 convert_element_type.100
  236.9 1.0 convolution_convert_fusion.2
  238.0 8.6 %fusion.11 = bf16[256,3072]{1,0:T(8,128)(2,1)} fusion(f32[256,4608]{1,0:T(8,128)} %copy-done.3), kind=kLoop, calls=%fused_computation.15 | loop fusion | flops 51118080 | bytes 4718592 | tf_op jit(solution)/shard_map/convert_element_type | solution.py:64
  246.7 8.3 %all-gather.5.cloned.1.call-done = bf16[1024,512]{0,1:T(8,128)(2,1)} async-done(((bf16[256,512]{0,1:T(8,128)(2,1)}), bf16[1024,512]{0,1:T(8,128)(2,1)}) %all-gather.5.cloned.1.call-update) | async-done | bytes 1048592 | tf_op jit(solution)/shard_map/all_gather | solution.py:78
  255.0 4.7 convolution_convert_fusion.1
  259.7 4.7 all-to-all-start.1
  264.4 72.0 %all-gather.7.cloned.1.call-done = bf16[1024,3072]{1,0:T(8,128)(2,1)} async-done(((bf16[256,3072]{1,0:T(8,128)(2,1)}), bf16[1024,3072]{1,0:T(8,128)(2,1)}) %all-gather.7.cloned.1.call-update) | async-done | bytes 6291472 | tf_op jit(solution)/shard_map/all_gather | solution.py:83
  336.4 15.5 %convolution_convert_fusion = bf16[1024,1536]{1,0:T(8,128)(2,1)} fusion(bf16[1024,3072]{1,0:T(8,128)(2,1)} %all-gather.7.cloned.1.call-done, bf16[3072,1536]{1,0:T(8,128)(2,1)} %param.17), kind=kOutput, calls=%fused_computation.11 | convolution fusion | flops 9665249280 | bytes 18874368 | tf_op jit(solution)/shard_map/dot_general | solution.py:82
  352.0 4.9 all-to-all-start.2
  356.9 6.0 %copy.36 = bf16[256,4,1536]{2,1,0:T(4,128)(2,1)} copy(bf16[256,4,1536]{2,0,1:T(8,128)(2,1)} %bitcast.15) | data formatting | bytes 6291456 | tf_op jit(solution)/shard_map/all_to_all | solution.py:88
  362.9 6.9 %stack.9 = bf16[1,256,6144]{2,1,0:T(8,128)(2,1)} reshape(bf16[256,4,1536]{2,1,0:T(4,128)(2,1)} %copy.36) | data formatting | bytes 6291456 | tf_op jit(solution)/shard_map/stack | solution.py:95
  369.8 24.0 %all-to-all-done.2 = bf16[4,256,1536]{2,1,0:T(8,128)(2,1)} async-done(((bf16[4,256,1536]{2,1,0:T(8,128)(2,1)}), bf16[4,256,1536]{2,1,0:T(8,128)(2,1)}, u32[]{:S(2)}, u32[]{:S(2)}) %all-to-all-start.2) | async-done | bytes 3145760 | tf_op jit(solution)/shard_map/all_to_all | solution.py:91
  393.8 6.0 %copy.37 = bf16[256,4,1536]{2,1,0:T(4,128)(2,1)} copy(bf16[256,4,1536]{2,0,1:T(8,128)(2,1)} %bitcast.17) | data formatting | bytes 6291456 | tf_op jit(solution)/shard_map/all_to_all | solution.py:91
  399.8 6.9 %stack.10 = bf16[1,256,6144]{2,1,0:T(8,128)(2,1)} reshape(bf16[256,4,1536]{2,1,0:T(4,128)(2,1)} %copy.37) | data formatting | bytes 6291456 | tf_op jit(solution)/shard_map/stack | solution.py:95
  406.7 6.1 %pad_maximum_fusion = bf16[2,256,6144]{2,1,0:T(8,128)(2,1)} fusion(bf16[1,256,6144]{2,1,0:T(8,128)(2,1)} %stack.10, bf16[1,256,6144]{2,1,0:T(8,128)(2,1)} %stack.9), kind=kLoop, calls=%fused_computation.5 | loop fusion | flops 3145728 | bytes 12582912 | tf_op jit(solution)/shard_map/stack | solution.py:95
  412.9 118.2 %reduce-scatter.5.cloned.1.call-done = bf16[2,256,768]{2,1,0:T(8,128)(2,1)} async-done(((bf16[2,256,6144]{2,1,0:T(8,128)(2,1)}), bf16[2,256,768]{2,1,0:T(8,128)(2,1)}) %reduce-scatter.5.cloned.1.call-update) | async-done | bytes 786448 | tf_op jit(solution)/shard_map/reduce_scatter | solution.py:97
  531.0 1.2 convert_element_type.110
  532.3 1.0 fusion.23
  (52 shorter events, 7.5 us)
Async XLA Ops:
  6.5 248.4 %copy-start = (bf16[512,1536]{1,0:T(8,128)(2,1)S(1)}, bf16[512,1536]{1,0:T(8,128)(2,1)}, u32[]{:S(2)}) copy-start(bf16[512,1536]{1,0:T(8,128)(2,1)} %param.16) | copy-start | bytes 4718596
  6.5 65.7 %all-gather.9.cloned.1.call-start = ((), (), s32[]{:S(2)}) async-start(), calls=%async_computation.9 | async-start | bytes 3538944 | tf_op jit(solution)/shard_map/all_gather | solution.py:37
  76.9 2.8 copy-start.2
  83.6 41.7 %all-to-all-start = ((bf16[256,4,1536]{0,2,1:T(8,128)(2,1)}), bf16[256,4,1536]{0,2,1:T(8,128)(2,1)}, u32[]{:S(2)}, u32[]{:S(2)}) async-start(bf16[256,4,1536]{0,2,1:T(8,128)(2,1)} %multiply_convert_fusion), calls=%async_computation | async-start | bytes 6291456 | tf_op jit(solution)/shard_map/all_to_all | solution.py:49
  88.3 140.2 %reduce-scatter.3.cloned.1.call-start = ((), (), s32[]{:S(2)}) async-start(), calls=%async_computation.5 | async-start | bytes 11796480 | tf_op jit(solution)/shard_map/reduce_scatter | solution.py:55
  152.6 0.7 copy-start.7
  152.6 0.7 copy-start.8
  152.6 102.3 %all-gather.5.cloned.1.call-start = ((), (), s32[]{:S(2)}) async-start(), calls=%async_computation.6 | async-start | bytes 1310720 | tf_op jit(solution)/shard_map/all_gather | solution.py:78
  229.6 2.5 slice-start
  234.5 2.1 copy-start.3
  238.0 98.4 %all-gather.7.cloned.1.call-start = ((), (), s32[]{:S(2)}) async-start(), calls=%async_computation.7 | async-start | bytes 7864320 | tf_op jit(solution)/shard_map/all_gather | solution.py:83
  259.7 92.3 %all-to-all-start.1 = ((bf16[4,256,1536]{2,1,0:T(8,128)(2,1)}), bf16[4,256,1536]{2,1,0:T(8,128)(2,1)}, u32[]{:S(2)}, u32[]{:S(2)}) async-start(bf16[4,256,1536]{2,1,0:T(8,128)(2,1)} %bitcast.83), calls=%async_computation.2 | async-start | bytes 6291456 | tf_op jit(solution)/shard_map/all_to_all | solution.py:88
  352.0 41.8 %all-to-all-start.2 = ((bf16[4,256,1536]{2,1,0:T(8,128)(2,1)}), bf16[4,256,1536]{2,1,0:T(8,128)(2,1)}, u32[]{:S(2)}, u32[]{:S(2)}) async-start(bf16[4,256,1536]{2,1,0:T(8,128)(2,1)} %bitcast.82), calls=%async_computation.3 | async-start | bytes 6291456 | tf_op jit(solution)/shard_map/all_to_all | solution.py:91
  356.8 174.2 %reduce-scatter.5.cloned.1.call-start = ((), (), s32[]{:S(2)}) async-start(), calls=%async_computation.8 | async-start | bytes 7077888 | tf_op jit(solution)/shard_map/reduce_scatter | solution.py:97
  412.8 119.4 %copy-start.4 = (bf16[1,256,768]{2,1,0:T(8,128)(2,1)S(1)}, bf16[1,256,768]{2,1,0:T(8,128)(2,1)}, u32[]{:S(2)}) copy-start(bf16[1,256,768]{2,1,0:T(8,128)(2,1)} %param.10) | copy-start | bytes 1179652
  412.8 119.5 %copy-start.5 = (s32[1,256,768]{2,1,0:T(8,128)S(1)}, s32[1,256,768]{2,1,0:T(8,128)}, u32[]{:S(2)}) copy-start(s32[1,256,768]{2,1,0:T(8,128)} %param.19) | copy-start | bytes 2359300
  412.8 119.5 %copy-start.6 = (s32[1,256,768]{2,1,0:T(8,128)S(1)}, s32[1,256,768]{2,1,0:T(8,128)}, u32[]{:S(2)}) copy-start(s32[1,256,768]{2,1,0:T(8,128)} %param.18) | copy-start | bytes 2359300
  412.9 120.4 %copy-start.1 = (bf16[512,1536]{1,0:T(8,128)(2,1)S(1)}, bf16[512,1536]{1,0:T(8,128)(2,1)}, u32[]{:S(2)}) copy-start(bf16[512,1536]{1,0:T(8,128)(2,1)} %param.16) | copy-start | bytes 4718596
Sparse Core Ops, SparseCore 0:
  9.5 62.7 all-gather.8
  152.8 75.6 reduce-scatter.2
  238.1 16.8 all-gather.4
  256.4 79.9 all-gather.6
  413.0 117.9 reduce-scatter.4
